TPU v7x, 32 devices: a whole 2x2x4 slice. The times are simulated.
32 devices in a mesh: section: 2 (over y), dp: 4 (over x, core), mp: 4 (over z).
Axes of the slice: x: 2, y: 2, z: 4, core: 2. Of those that a mesh axis runs over, the one named last changes fastest.
Arguments:
- activations: bfloat16 [2, 256, 4096], P(None, 'dp'), may hold values from -6 to 6
- cotangent: bfloat16 [2, 256, 4096], P(None, 'dp'), may hold values from -6 to 6
- norm_gain: float32 [2, 4096], P('section'), may hold values from 0.1 to 1.9
- w_up: bfloat16 [2, 4096, 8192], P('section', 'dp', 'mp'), may hold values from -0.09375 to 0.09375
- w_down: bfloat16 [2, 4096, 8192], P('section', 'dp', 'mp'), may hold values from -0.0625 to 0.0625
- gram_left: float32 [2, 128, 512, 512], P('section', ('dp', 'mp')), as said below
- gram_right: float32 [2, 128, 512, 512], P('section', ('dp', 'mp')), as said below
- root_left: bfloat16 [2, 128, 512, 512], P('section', ('dp', 'mp'))
- root_right: bfloat16 [2, 128, 512, 512], P('section', ('dp', 'mp'))
- owner_slot: int32 [2, 16, 8], replicated, may hold values from 0 to 127, as said below
- eighth: int32 [2, 16, 8], replicated, may hold values from 0 to 7, as said below
- refresh_phase: int32 [1], replicated, may hold values from 0 to 999999
Outputs:
- new_gram_left: float32 [2, 128, 512, 512], P('section', ('dp', 'mp'))
- new_gram_right: float32 [2, 128, 512, 512], P('section', ('dp', 'mp'))
- new_root_left: bfloat16 [2, 128, 512, 512], P('section', ('dp', 'mp'))
- new_root_right: bfloat16 [2, 128, 512, 512], P('section', ('dp', 'mp'))
- update_blocks: bfloat16 [2, 128, 512, 512], P('section', ('dp', 'mp'))
Inputs may be any that keep to these rules, and one draw needn't show every extreme that they name: `owner_slot`: for each section, a permutation of the 128 slots; the block of flat index f = i * 8 + j goes to a slot t with (t // 8) % (4) == f // 32. `eighth`: in each section and each run of 32 consecutive flat block indices, every value is taken by exactly 4 blocks. `gram_left`: symmetric positive definite. `gram_right`: symmetric positive definite.
All inputs are finite; a program needn't handle non-finite values.
Results may differ from a plain program's by a relative error of at most 0.025.
Values may be sent and summed in bfloat16 or wider, within the bound.
A program may use at most 192 MiB of HBM per device.

v0:
```python
import math
import jax
import jax.numpy as jnp
from jax import lax
from jax.sharding import PartitionSpec as P

BLK = 512
ITERS = 2
norm_epsilon = 1e-05
decay_rate = 0.9
ridge_shift = 0.001
highest = lax.Precision.HIGHEST


def passed_along(block, axis, distance):
    devices = range(lax.axis_size(axis))
    route = [(i - distance, i) for i in devices if i - distance in devices]
    return lax.ppermute(block, axis, route)


def normalize_values(values, gain_row):
    inverse_rms = lax.rsqrt(jnp.mean(values * values, axis=-1, keepdims=True) + norm_epsilon)
    return values * inverse_rms * gain_row


def silu_slope(pre_act):
    sigmoid_values = jax.nn.sigmoid(pre_act)
    return sigmoid_values * (1.0 + pre_act * (1.0 - sigmoid_values))


def inverse_root(matrix):
    matrix_order = matrix.shape[-1]
    identity = jnp.eye(matrix_order, dtype=jnp.float32)
    shifted = matrix + ridge_shift * identity
    factor = 2.5 / jnp.sqrt(jnp.sum(shifted * shifted))
    iterate = jnp.power(factor, 0.25) * identity
    moment = factor * shifted
    for sweep_no in range(ITERS):
        step_mat = 1.25 * identity - 0.25 * moment
        square = jnp.dot(step_mat, step_mat, precision=highest)
        fourth = jnp.dot(square, square, precision=highest)
        moment = jnp.dot(fourth, moment, precision=highest)
        iterate = jnp.dot(iterate, step_mat, precision=highest)
    return iterate


def forward_layer(inputs, gain_row, up_rows, down_rows):
    values = inputs.astype(jnp.float32)
    normed = normalize_values(values, gain_row).astype(jnp.bfloat16)
    pre_act = jnp.dot(normed, up_rows, preferred_element_type=jnp.float32)
    hidden = jax.nn.silu(pre_act).astype(jnp.bfloat16)
    partial_value = lax.dot_general(
        hidden, down_rows, (((1,), (1,)), ((), ())), preferred_element_type=jnp.float32
    )
    branch = lax.psum(partial_value.astype(jnp.bfloat16), "mp").astype(jnp.float32)
    output = (values + branch).astype(jnp.bfloat16)
    return (output, pre_act, hidden)


def backward_layer(grad_output, inputs, pre_act, gain_row, up_rows, down_rows):
    grad_hidden = jnp.dot(grad_output, down_rows, preferred_element_type=jnp.float32)
    grad_pre = (grad_hidden * silu_slope(pre_act)).astype(jnp.bfloat16)
    partial_value = lax.dot_general(
        grad_pre, up_rows, (((1,), (1,)), ((), ())), preferred_element_type=jnp.float32
    )
    grad_normed = lax.psum(partial_value.astype(jnp.bfloat16), "mp").astype(jnp.float32)
    values = inputs.astype(jnp.float32)
    unused, pullback = jax.vjp(lambda values_in: normalize_values(values_in, gain_row), values)
    grad_values = pullback(grad_normed)[0]
    return (grad_output.astype(jnp.float32) + grad_values).astype(jnp.bfloat16)


def store_row(stack, entry, slot_index, is_valid):
    return jnp.where(is_valid, lax.dynamic_update_index_in_dim(stack, entry, slot_index, 0), stack)


def on_device(
    activations,
    cotangent,
    norm_gain,
    w_up,
    w_down,
    gram_left,
    gram_right,
    root_left,
    root_right,
    owner_slot,
    eighth,
    refresh_phase,
):
    section_no = lax.axis_index("section")
    dp_no = lax.axis_index("dp")
    mp_no = lax.axis_index("mp")
    section_total = lax.axis_size("section")
    dp_count = lax.axis_size("dp")
    mp_count = lax.axis_size("mp")
    micro_count, row_count, model_width = activations.shape
    gain_row = norm_gain[0]
    up_full, down_full = (
        lax.all_gather(w_up[0], "dp", axis=0, tiled=True),
        lax.all_gather(w_down[0], "dp", axis=0, tiled=True),
    )
    shard_ff = up_full.shape[1]
    tick_total = micro_count + section_total - 1
    inputs_all = jnp.zeros((micro_count, row_count, model_width), jnp.bfloat16)
    pre_all = jnp.zeros((micro_count, row_count, shard_ff), jnp.float32)
    hidden_all = jnp.zeros((micro_count, row_count, shard_ff), jnp.bfloat16)
    received = jnp.zeros((row_count, model_width), jnp.bfloat16)
    is_first = section_no == 0
    for tick_no in range(tick_total):
        batch_no = tick_no - section_no
        is_valid = (batch_no >= 0) & (batch_no < micro_count)
        slot_index = jnp.clip(batch_no, 0, micro_count - 1)
        inputs = jnp.where(is_first, activations[min(tick_no, micro_count - 1)], received)
        output, pre_act, hidden = forward_layer(inputs, gain_row, up_full, down_full)
        inputs_all = store_row(inputs_all, inputs, slot_index, is_valid)
        pre_all = store_row(pre_all, pre_act, slot_index, is_valid)
        hidden_all = store_row(hidden_all, hidden, slot_index, is_valid)
        if tick_no < tick_total - 1:
            received = passed_along(output, "section", 1)
    grad_all = jnp.zeros((micro_count, row_count, model_width), jnp.bfloat16)
    received = jnp.zeros((row_count, model_width), jnp.bfloat16)
    is_last = section_no == section_total - 1
    for tick_no in range(tick_total):
        batch_no = tick_no - (section_total - 1 - section_no)
        is_valid = (batch_no >= 0) & (batch_no < micro_count)
        slot_index = jnp.clip(batch_no, 0, micro_count - 1)
        grad_output = jnp.where(is_last, cotangent[min(tick_no, micro_count - 1)], received)
        inputs = lax.dynamic_index_in_dim(inputs_all, slot_index, 0, keepdims=False)
        pre_act = lax.dynamic_index_in_dim(pre_all, slot_index, 0, keepdims=False)
        grad_all = store_row(grad_all, grad_output, slot_index, is_valid)
        grad_input = backward_layer(grad_output, inputs, pre_act, gain_row, up_full, down_full)
        if tick_no < tick_total - 1:
            received = passed_along(grad_input, "section", -1)
    token_count = micro_count * row_count
    block_rows = shard_ff // BLK
    block_cols = model_width // BLK
    group_size = block_rows * block_cols
    per_dev = group_size // dp_count
    hidden_flat = hidden_all.reshape(token_count, block_rows, BLK)
    grad_flat = grad_all.reshape(token_count, block_cols, BLK)
    section_owner = lax.dynamic_index_in_dim(owner_slot, section_no, 0, keepdims=False)
    local_owner = lax.dynamic_slice_in_dim(
        section_owner, mp_no * block_rows, block_rows, 0
    ).reshape(-1)
    local_slot = local_owner // (mp_count * per_dev) * per_dev + local_owner % per_dev
    block_of_slot = jnp.argsort(local_slot)
    row_of_slot = block_of_slot // block_cols
    col_of_slot = block_of_slot % block_cols
    hidden_slots = jnp.take(hidden_flat, row_of_slot, axis=1)
    grad_slots = jnp.take(grad_flat, col_of_slot, axis=1)
    hidden_recv, grad_recv = (
        lax.all_to_all(hidden_slots, "dp", split_axis=1, concat_axis=0, tiled=True),
        lax.all_to_all(grad_slots, "dp", split_axis=1, concat_axis=0, tiled=True),
    )
    hidden_in = hidden_recv.reshape(dp_count, token_count, per_dev, BLK)
    grad_in = grad_recv.reshape(dp_count, token_count, per_dev, BLK)
    products = jnp.einsum("snbk,snbl->sbkl", hidden_in, grad_in, preferred_element_type=jnp.float32)
    rounded = lax.optimization_barrier(products.astype(jnp.bfloat16)).astype(jnp.float32)
    summed = jnp.sum(rounded, axis=0)
    scaled = summed * (1.0 / math.sqrt(token_count * dp_count))
    left_new = (
        decay_rate * gram_left[0]
        + jnp.einsum("sij,skj->sik", scaled, scaled, precision=highest) / BLK
    )
    right_new = (
        decay_rate * gram_right[0]
        + jnp.einsum("sji,sjk->sik", scaled, scaled, precision=highest) / BLK
    )
    phase_now = refresh_phase[0] % 8
    section_eighth = lax.dynamic_index_in_dim(eighth, section_no, 0, keepdims=False)
    local_eighth = lax.dynamic_slice_in_dim(
        section_eighth, mp_no * block_rows, block_rows, 0
    ).reshape(-1)
    is_due = jnp.take(local_eighth, block_of_slot) == phase_now
    my_due = lax.dynamic_slice_in_dim(is_due, dp_no * per_dev, per_dev)

    def refresh_slot(operands):
        return lax.cond(
            operands[0],
            lambda ops: (
                inverse_root(ops[1]).astype(jnp.bfloat16),
                inverse_root(ops[2]).astype(jnp.bfloat16),
            ),
            lambda ops: (ops[3], ops[4]),
            operands,
        )

    roots_l, roots_r = lax.map(
        refresh_slot, (my_due, left_new, right_new, root_left[0], root_right[0])
    )
    grad_low = scaled.astype(jnp.bfloat16)
    inner_product = jnp.einsum(
        "sij,sjk->sik", grad_low, roots_r, preferred_element_type=jnp.float32
    ).astype(jnp.bfloat16)
    update = jnp.einsum(
        "sij,sjk->sik", roots_l, inner_product, preferred_element_type=jnp.float32
    ).astype(jnp.bfloat16)
    return (left_new[None], right_new[None], roots_l[None], roots_r[None], update[None])


def solution(mesh):
    return jax.shard_map(
        on_device,
        mesh=mesh,
        in_specs=(
            P(None, "dp", None),
            P(None, "dp", None),
            P("section", None),
            P("section", "dp", "mp"),
            P("section", "dp", "mp"),
            P("section", ("dp", "mp"), None, None),
            P("section", ("dp", "mp"), None, None),
            P("section", ("dp", "mp"), None, None),
            P("section", ("dp", "mp"), None, None),
            P(),
            P(),
            P(),
        ),
        out_specs=(
            P("section", ("dp", "mp"), None, None),
            P("section", ("dp", "mp"), None, None),
            P("section", ("dp", "mp"), None, None),
            P("section", ("dp", "mp"), None, None),
            P("section", ("dp", "mp"), None, None),
        ),
        check_vma=False,
    )
```

profile of v0, /device:TPU:0, one launch (start us, length us, event | category | flops | bytes accessed | tf_op | source)
XLA Modules:
  0.0 786.2 jit_solution(6627781290026587765)
XLA Ops:
  9.0 109.2 %all-gather.5.cloned.1.call-done = bf16[1,4096,2048]{2,1,0:T(8,128)(2,1)} async-done(((bf16[1,1024,2048]{2,1,0:T(8,128)(2,1)}), bf16[1,4096,2048]{2,1,0:T(8,128)(2,1)}) %all-gather.5.cloned.1.call-update) | async-done | bytes 16777232 | tf_op jit(solution)/shard_map/all_gather | solution.py:100
  118.3 8.9 %bitcast_dynamic-update-slice_fusion.1 = (bf16[2,64,2048]{2,1,0:T(8,128)(2,1)S(1)}, f32[64,2048]{1,0:T(8,128)S(1)}) fusion(bf16[2,64,2048]{2,1,0:T(8,128)(2,1)S(1)} %broadcast_in_dim.113, s32[]{:T(128)S(6)} %min.19, pred[]{:T(512)S(6)} %and.63, bf16[1,4096,2048]{2,1,0:T(8,128)(2,1)} %all-gather.5.cloned.1.call-done, f32[4096]{0:T(1024)S(1)} %bitcast.238, ...), kind=kOutput, calls=%fused_computation.236 | convolution fusion | flops 1075838976 | bytes 18104838 | tf_op jit(solution)/shard_map/dot_general | solution.py:50
  127.2 98.5 %all-gather.7.cloned.1.call-done = bf16[1,4096,2048]{2,1,0:T(8,128)(2,1)} async-done(((bf16[1,1024,2048]{2,1,0:T(8,128)(2,1)}), bf16[1,4096,2048]{2,1,0:T(8,128)(2,1)}) %all-gather.7.cloned.1.call-update) | async-done | bytes 16777232 | tf_op jit(solution)/shard_map/all_gather | solution.py:101
  225.7 11.7 %fusion.108 = bf16[64,4096]{1,0:T(8,128)(2,1)} fusion(bf16[1,4096,2048]{2,1,0:T(8,128)(2,1)} %all-gather.7.cloned.1.call-done, f32[64,2048]{1,0:T(8,128)S(1)} %get-tuple-element.165), kind=kOutput, calls=%fused_computation.130 | convolution fusion | flops 1074659328 | bytes 17825792 | tf_op jit(solution)/shard_map/dot_general | solution.py:52
  237.5 38.7 %all-reduce.5.cloned.1.call-done = bf16[64,4096]{1,0:T(8,128)(2,1)} async-done(((bf16[64,4096]{1,0:T(8,128)(2,1)}), bf16[64,4096]{1,0:T(8,128)(2,1)}) %all-reduce.5.cloned.1.call-update) | async-done | bytes 524304 | tf_op jit(solution)/shard_map/psum | solution.py:55
  277.4 3.6 collective-permute-start
  281.3 9.8 %collective-permute-done = bf16[64,4096]{1,0:T(8,128)(2,1)S(1)} collective-permute-done((bf16[64,4096]{1,0:T(8,128)(2,1)S(1)}, bf16[64,4096]{1,0:T(8,128)(2,1)S(1)}, u32[]{:S(2)}, u32[]{:S(2)}) %collective-permute-start) | collective-permute-done | bytes 524320 | tf_op jit(solution)/shard_map/ppermute | solution.py:18
  291.6 9.7 %fusion.198 = (bf16[2,64,2048]{2,1,0:T(8,128)(2,1)S(1)}, f32[64,2048]{1,0:T(8,128)}) fusion(bf16[2,64,2048]{2,1,0:T(8,128)(2,1)S(1)} %get-tuple-element.164, s32[]{:T(128)S(6)} %min.20, pred[]{:T(512)S(6)} %and.64, bf16[1,4096,2048]{2,1,0:T(8,128)(2,1)} %all-gather.5.cloned.1.call-done, bf16[64,4096]{1,0:T(8,128)(2,1)S(1)} %get-tuple-element.148, ...), kind=kOutput, calls=%fused_computation.235 | convolution fusion | flops 1075576832 | bytes 18366980 | tf_op jit(solution)/shard_map/dot_general | solution.py:50
  301.3 12.1 %fusion.111 = bf16[64,4096]{1,0:T(8,128)(2,1)} fusion(bf16[1,4096,2048]{2,1,0:T(8,128)(2,1)} %all-gather.7.cloned.1.call-done, f32[64,2048]{1,0:T(8,128)} %get-tuple-element.167), kind=kOutput, calls=%fused_computation.131 | convolution fusion | flops 1074659328 | bytes 17825792 | tf_op jit(solution)/shard_map/dot_general | solution.py:52
  316.2 36.6 %all-reduce.7.cloned.1.call-done = bf16[64,4096]{1,0:T(8,128)(2,1)} async-done(((bf16[64,4096]{1,0:T(8,128)(2,1)}), bf16[64,4096]{1,0:T(8,128)(2,1)}) %all-reduce.7.cloned.1.call-update) | async-done | bytes 524304 | tf_op jit(solution)/shard_map/psum | solution.py:55
  354.0 3.7 collective-permute-start.1
  362.7 5.0 collective-permute-done.1
  368.1 9.0 %fusion.197 = (bf16[2,64,2048]{2,1,0:T(8,128)(2,1)S(1)}, f32[64,2048]{1,0:T(8,128)S(1)}) fusion(bf16[2,64,2048]{2,1,0:T(8,128)(2,1)S(1)} %copy-done.4, s32[]{:T(128)S(6)} %min.21, pred[]{:T(512)S(6)} %and.65, bf16[1,4096,2048]{2,1,0:T(8,128)(2,1)} %all-gather.5.cloned.1.call-done, bf16[64,4096]{1,0:T(8,128)(2,1)S(1)} %get-tuple-element.146, ...), kind=kOutput, calls=%fused_computation.233 | convolution fusion | flops 1075576832 | bytes 18366980 | tf_op jit(solution)/shard_map/dot_general | solution.py:50
  379.9 15.7 %fusion.102 = bf16[64,4096]{1,0:T(8,128)(2,1)} fusion(bf16[1,4096,2048]{2,1,0:T(8,128)(2,1)} %all-gather.5.cloned.1.call-done, bf16[1,4096,2048]{2,1,0:T(8,128)(2,1)} %all-gather.7.cloned.1.call-done, f32[2,64,2048]{2,1,0:T(8,128)} %fusion.180, s32[]{:T(128)S(6)} %min.22, bf16[2,64,4096]{2,1,0:T(8,128)(2,1)S(1)} %copy-done.2, pred[]{:T(512)S(6)} %eq.60), kind=kOutput, calls=%fused_computation.128 | convolution fusion | flops 2149187584 | bytes 35127300 | tf_op jit(solution)/shard_map/dot_general | solution.py:63
  397.6 37.3 %all-reduce.9.cloned.1.call-done = bf16[64,4096]{1,0:T(8,128)(2,1)} async-done(((bf16[64,4096]{1,0:T(8,128)(2,1)}), bf16[64,4096]{1,0:T(8,128)(2,1)}) %all-reduce.9.cloned.1.call-update) | async-done | bytes 524304 | tf_op jit(solution)/shard_map/psum | solution.py:66
  440.4 12.2 %collective-permute-done.2 = bf16[64,4096]{1,0:T(8,128)(2,1)} collective-permute-done((bf16[64,4096]{1,0:T(8,128)(2,1)S(1)}, bf16[64,4096]{1,0:T(8,128)(2,1)}, u32[]{:S(2)}, u32[]{:S(2)}) %collective-permute-start.2) | collective-permute-done | bytes 524320 | tf_op jit(solution)/shard_map/ppermute | solution.py:18
  454.9 15.8 %fusion.105 = bf16[64,4096]{1,0:T(8,128)(2,1)} fusion(bf16[1,4096,2048]{2,1,0:T(8,128)(2,1)} %all-gather.5.cloned.1.call-done, bf16[64,4096]{1,0:T(8,128)(2,1)S(1)} %get-tuple-element.144, bf16[1,4096,2048]{2,1,0:T(8,128)(2,1)} %all-gather.7.cloned.1.call-done, f32[2,64,2048]{2,1,0:T(8,128)} %fusion.180, s32[]{:T(128)S(6)} %min.23), kind=kOutput, calls=%fused_computation.129 | convolution fusion | flops 2148925440 | bytes 35127300 | tf_op jit(solution)/shard_map/dot_general | solution.py:63
  475.8 4.7 select_bitcast_fusion.1
  480.5 4.8 all-to-all-start
  485.4 22.8 %all-reduce.11.cloned.1.call-done = bf16[64,4096]{1,0:T(8,128)(2,1)} async-done(((bf16[64,4096]{1,0:T(8,128)(2,1)}), bf16[64,4096]{1,0:T(8,128)(2,1)}) %all-reduce.11.cloned.1.call-update) | async-done | bytes 524304 | tf_op jit(solution)/shard_map/psum | solution.py:66
  512.2 13.3 %collective-permute-done.3 = bf16[64,4096]{1,0:T(8,128)(2,1)S(1)} collective-permute-done((bf16[64,4096]{1,0:T(8,128)(2,1)S(1)}, bf16[64,4096]{1,0:T(8,128)(2,1)S(1)}, u32[]{:S(2)}, u32[]{:S(2)}) %collective-permute-start.3) | collective-permute-done | bytes 524320 | tf_op jit(solution)/shard_map/ppermute | solution.py:18
  532.3 4.7 select_bitcast_fusion
  537.0 5.0 all-to-all-start.1
  542.1 6.4 copy.34
  548.6 41.7 %all-to-all-done.1 = bf16[128,32,512]{2,0,1:T(8,128)(2,1)} async-done(((bf16[128,32,512]{2,0,1:T(8,128)(2,1)}), bf16[128,32,512]{2,0,1:T(8,128)(2,1)}, u32[]{:S(2)}, u32[]{:S(2)}) %all-to-all-start.1) | async-done | bytes 4194336 | tf_op jit(solution)/shard_map/all_to_all | solution.py:154
  590.2 10.9 %convolution_convert_fusion.2 = bf16[4,8,512,512]{3,2,1,0:T(8,128)(2,1)} fusion(bf16[4,128,8,512]{1,3,2,0:T(8,128)(2,1)} %bitcast.236, bf16[4,128,8,512]{3,1,2,0:T(8,128)(2,1)} %bitcast.37), kind=kOutput, calls=%fused_computation.120 | convolution fusion | flops 2155872256 | bytes 25165824 | tf_op jit(solution)/shard_map/snbk,snbl->sbkl/dot_general | solution.py:158
  601.1 9.6 %convert_reduce_fusion = f32[8,512,512]{2,1,0:T(8,128)S(1)} fusion(bf16[4,8,512,512]{3,2,1,0:T(8,128)(2,1)} %convolution_convert_fusion.2), kind=kLoop, calls=%fused_computation.101 | loop fusion | flops 14680064 | bytes 25165824 | tf_op jit(solution)/shard_map/reduce_sum | solution.py:160
  610.7 19.7 %bitcast_add_fusion = f32[8,512,512]{2,1,0:T(8,128)} fusion(f32[1,8,512,512]{3,2,1,0:T(8,128)} %param.22, f32[8,512,512]{2,1,0:T(8,128)S(1)} %convert_reduce_fusion), kind=kOutput, calls=%fused_computation.121 | convolution fusion | flops 12893290496 | bytes 25165824 | tf_op jit(solution)/shard_map/sji,sjk->sik/dot_general | solution.py:168
  630.4 17.6 %bitcast_add_fusion.1 = f32[8,512,512]{2,1,0:T(8,128)} fusion(f32[1,8,512,512]{3,2,1,0:T(8,128)} %param.21, f32[8,512,512]{2,1,0:T(8,128)S(1)} %convert_reduce_fusion), kind=kOutput, calls=%fused_computation.122 | convolution fusion | flops 12893290496 | bytes 25165824 | tf_op jit(solution)/shard_map/sij,skj->sik/dot_general | solution.py:164
  648.0 118.6 %while.12 = (s32[]{:T(128)}, bf16[8,512,512]{2,1,0:T(8,128)(2,1)}, bf16[8,512,512]{2,1,0:T(8,128)(2,1)}, pred[8]{0:T(512)(128)(4,1)S(1)}, bf16[8,512,512]{2,1,0:...) while((s32[]{:T(128)}, bf16[8,512,512]{2,1,0:T(8,128)(2,1)}, ...), condition=%wide.region_18.19_spmd, body=%wide.region_13.18_spmd.sunk | while | flops 16121331712 | bytes 28315412 | solution.py:189
  660.1 31.2 %conditional.2 = (bf16[1,512,512]{2,1,0:T(8,128)(2,1)S(1)}, bf16[1,512,512]{2,1,0:T(8,128)(2,1)S(1)}) conditional(s32[]{:T(128)} %bitcast.230, (bf16[8,512,512]{2,1,0:T(8,128)(2,1)}, s32[]{:T(128)}, bf16[8,512,512]{2,1,0:T(8,128)(2,1)}) %tuple.65, (f32[8,512,512]{2,1,0:T(8,128)}, s32[]{:T(128)}, f32[8,512,512]{2,1,0:T(8,128)}) %tuple.66), branch_computations={%region_14.14_spmd, %region_15.17_spmd} | conditional | flops 16121331712 | bytes 26217596 | solution.py:179
  663.3 3.6 fusion.6
  668.8 3.1 select_subtract_fusion
  677.7 3.7 fusion.3
  683.2 3.1 select_subtract_fusion.2
  686.4 3.1 fusion.14
  693.6 31.1 %conditional.2 = (bf16[1,512,512]{2,1,0:T(8,128)(2,1)S(1)}, bf16[1,512,512]{2,1,0:T(8,128)(2,1)S(1)}) conditional(s32[]{:T(128)} %bitcast.230, (bf16[8,512,512]{2,1,0:T(8,128)(2,1)}, s32[]{:T(128)}, bf16[8,512,512]{2,1,0:T(8,128)(2,1)}) %tuple.65, (f32[8,512,512]{2,1,0:T(8,128)}, s32[]{:T(128)}, f32[8,512,512]{2,1,0:T(8,128)}) %tuple.66), branch_computations={%region_14.14_spmd, %region_15.17_spmd} | conditional | flops 16121331712 | bytes 26217596 | solution.py:179
  696.8 3.6 fusion.6
  702.3 3.1 select_subtract_fusion
  711.1 3.6 fusion.3
  716.6 3.1 select_subtract_fusion.2
  727.1 31.1 %conditional.2 = (bf16[1,512,512]{2,1,0:T(8,128)(2,1)S(1)}, bf16[1,512,512]{2,1,0:T(8,128)(2,1)S(1)}) conditional(s32[]{:T(128)} %bitcast.230, (bf16[8,512,512]{2,1,0:T(8,128)(2,1)}, s32[]{:T(128)}, bf16[8,512,512]{2,1,0:T(8,128)(2,1)}) %tuple.65, (f32[8,512,512]{2,1,0:T(8,128)}, s32[]{:T(128)}, f32[8,512,512]{2,1,0:T(8,128)}) %tuple.66), branch_computations={%region_14.14_spmd, %region_15.17_spmd} | conditional | flops 16121331712 | bytes 26217596 | solution.py:179
  730.2 3.6 fusion.6
  735.7 3.1 select_subtract_fusion
  744.5 3.6 fusion.3
  750.0 3.1 select_subtract_fusion.2
  753.2 3.1 fusion.14
  766.6 12.3 %convert_bitcast_fusion = bf16[1,8,512,512]{3,2,1,0:T(8,128)(2,1)} fusion(bf16[8,512,512]{2,1,0:T(8,128)(2,1)} %get-tuple-element.120, bf16[8,512,512]{2,1,0:T(8,128)(2,1)} %get-tuple-element.121, f32[8,512,512]{2,1,0:T(8,128)} %copy-done), kind=kOutput, calls=%fused_computation.135 | convolution fusion | flops 4303355904 | bytes 20971520 | tf_op jit(solution)/shard_map/sij,sjk->sik/dot_general | solution.py:196
  (132 shorter events, 108.8 us)
Async XLA Ops:
  7.2 1.6 copy-start.1
  7.2 111.1 %copy-start.8 = (f32[1,4096]{1,0:T(1,128)S(1)}, f32[1,4096]{1,0:T(1,128)}, u32[]{:S(2)}) copy-start(f32[1,4096]{1,0:T(1,128)} %param.18) | copy-start | bytes 49156
  7.2 111.0 %all-gather.5.cloned.1.call-start = ((), (), s32[]{:S(2)}) async-start(), calls=%async_computation.6 | async-start | bytes 20971520 | tf_op jit(solution)/shard_map/all_gather | solution.py:100
  7.9 217.8 %all-gather.7.cloned.1.call-start = ((), (), s32[]{:S(2)}) async-start(), calls=%async_computation.7 | async-start | bytes 20971520 | tf_op jit(solution)/shard_map/all_gather | solution.py:101
  8.7 267.6 %all-reduce.5.cloned.1.call-start = ((), (), s32[]{:S(2)}) async-start(), calls=%async_computation.2 | async-start | bytes 1048576 | tf_op jit(solution)/shard_map/psum | solution.py:55
  127.2 110.2 %copy-start.7 = (f32[64,2048]{1,0:T(8,128)}, f32[64,2048]{1,0:T(8,128)S(1)}, u32[]{:S(2)}) copy-start(f32[64,2048]{1,0:T(8,128)S(1)} %get-tuple-element.165) | copy-start | bytes 1572868
  237.5 115.3 %all-reduce.7.cloned.1.call-start = ((), (), s32[]{:S(2)}) async-start(), calls=%async_computation.3 | async-start | bytes 1048576 | tf_op jit(solution)/shard_map/psum | solution.py:55
  277.4 13.6 %collective-permute-start = (bf16[64,4096]{1,0:T(8,128)(2,1)S(1)}, bf16[64,4096]{1,0:T(8,128)(2,1)S(1)}, u32[]{:S(2)}, u32[]{:S(2)}) collective-permute-start(bf16[64,4096]{1,0:T(8,128)(2,1)S(1)} %fusion.152), channel_id=1, source_target_pairs={{0,16},{1,17},{2,18},{3,19},{4,20},{5,21},{6,22},{7,23},{8,24},{9,... | collective-permute-start | bytes 1572872 | tf_op jit(solution)/shard_map/ppermute | solution.py:18
  301.3 13.2 %copy-start.3 = (bf16[2,64,2048]{2,1,0:T(8,128)(2,1)}, bf16[2,64,2048]{2,1,0:T(8,128)(2,1)S(1)}, u32[]{:S(2)}) copy-start(bf16[2,64,2048]{2,1,0:T(8,128)(2,1)S(1)} %get-tuple-element.166) | copy-start | bytes 1572868
  301.3 12.9 %copy-start.9 = (s32[2,16,8]{1,2,0:T(8,128)S(1)}, s32[2,16,8]{1,2,0:T(8,128)}, u32[]{:S(2)}) copy-start(s32[2,16,8]{1,2,0:T(8,128)} %param.26) | copy-start | bytes 3076
  301.3 12.9 %copy-start.10 = (s32[2,16,8]{1,2,0:T(8,128)S(1)}, s32[2,16,8]{1,2,0:T(8,128)}, u32[]{:S(2)}) copy-start(s32[2,16,8]{1,2,0:T(8,128)} %param.25) | copy-start | bytes 3076
  313.4 121.6 %all-reduce.9.cloned.1.call-start = ((), (), s32[]{:S(2)}) async-start(), calls=%async_computation.4 | async-start | bytes 1048576 | tf_op jit(solution)/shard_map/psum | solution.py:66
  352.8 15.3 %copy-start.4 = (bf16[2,64,2048]{2,1,0:T(8,128)(2,1)S(1)}, bf16[2,64,2048]{2,1,0:T(8,128)(2,1)}, u32[]{:S(2)}) copy-start(bf16[2,64,2048]{2,1,0:T(8,128)(2,1)} %copy-done.3) | copy-start | bytes 1572868
  354.0 13.6 %collective-permute-start.1 = (bf16[64,4096]{1,0:T(8,128)(2,1)S(1)}, bf16[64,4096]{1,0:T(8,128)(2,1)S(1)}, u32[]{:S(2)}, u32[]{:S(2)}) collective-permute-start(bf16[64,4096]{1,0:T(8,128)(2,1)S(1)} %fusion.144), channel_id=1, source_target_pairs={{0,16},{1,17},{2,18},{3,19},{4,20},{5,21},{6,22},{7,23},{8,24},{9,... | collective-permute-start | bytes 1572872 | tf_op jit(solution)/shard_map/ppermute | solution.py:18
  368.1 11.7 %copy-start.2 = (bf16[2,64,4096]{2,1,0:T(8,128)(2,1)S(1)}, bf16[2,64,4096]{2,1,0:T(8,128)(2,1)}, u32[]{:S(2)}) copy-start(bf16[2,64,4096]{2,1,0:T(8,128)(2,1)} %param.17) | copy-start | bytes 3145732
  377.2 0.8 copy-start.5
  395.6 112.6 %all-reduce.11.cloned.1.call-start = ((), (), s32[]{:S(2)}) async-start(), calls=%async_computation.5 | async-start | bytes 1048576 | tf_op jit(solution)/shard_map/psum | solution.py:66
  437.9 14.7 %collective-permute-start.2 = (bf16[64,4096]{1,0:T(8,128)(2,1)S(1)}, bf16[64,4096]{1,0:T(8,128)(2,1)}, u32[]{:S(2)}, u32[]{:S(2)}) collective-permute-start(bf16[64,4096]{1,0:T(8,128)(2,1)S(1)} %fusion.146), channel_id=1, source_target_pairs={{16,0},{17,1},{18,2},{19,3},{20,4},{21,5},{22,6},{23,7},{24,8},{25... | collective-permute-start | bytes 1572872 | tf_op jit(solution)/shard_map/ppermute | solution.py:18
  454.9 15.8 %copy-start.6 = (bf16[2,64,2048]{2,1,0:T(8,128)(2,1)S(1)}, bf16[2,64,2048]{2,1,0:T(8,128)(2,1)}, u32[]{:S(2)}) copy-start(bf16[2,64,2048]{2,1,0:T(8,128)(2,1)} %copy-done.5) | copy-start | bytes 1572868
  480.5 56.5 %all-to-all-start = ((bf16[128,32,512]{2,0,1:T(8,128)(2,1)}), bf16[128,32,512]{2,0,1:T(8,128)(2,1)}, u32[]{:S(2)}, u32[]{:S(2)}) async-start(bf16[128,32,512]{2,0,1:T(8,128)(2,1)} %select_bitcast_fusion.1), calls=%async_computation | async-start | bytes 8388608 | tf_op jit(solution)/shard_map/all_to_all | solution.py:153
  510.9 14.6 %collective-permute-start.3 = (bf16[64,4096]{1,0:T(8,128)(2,1)S(1)}, bf16[64,4096]{1,0:T(8,128)(2,1)S(1)}, u32[]{:S(2)}, u32[]{:S(2)}) collective-permute-start(bf16[64,4096]{1,0:T(8,128)(2,1)S(1)} %fusion.148), channel_id=1, source_target_pairs={{16,0},{17,1},{18,2},{19,3},{20,4},{21,5},{22,6},{23,7},{24,8},{25... | collective-permute-start | bytes 1572872 | tf_op jit(solution)/shard_map/ppermute | solution.py:18
  537.0 53.2 %all-to-all-start.1 = ((bf16[128,32,512]{2,0,1:T(8,128)(2,1)}), bf16[128,32,512]{2,0,1:T(8,128)(2,1)}, u32[]{:S(2)}, u32[]{:S(2)}) async-start(bf16[128,32,512]{2,0,1:T(8,128)(2,1)} %select_bitcast_fusion), calls=%async_computation.1 | async-start | bytes 8388608 | tf_op jit(solution)/shard_map/all_to_all | solution.py:154
  610.7 19.7 %copy-start = (f32[8,512,512]{2,1,0:T(8,128)}, f32[8,512,512]{2,1,0:T(8,128)S(1)}, u32[]{:S(2)}) copy-start(f32[8,512,512]{2,1,0:T(8,128)S(1)} %convert_reduce_fusion) | copy-start | bytes 25165828
Sparse Core Ops, SparseCore 0:
  9.5 108.6 all-gather.4
  119.8 105.8 all-gather.6
  237.6 38.6 all-reduce.4
  313.5 39.2 all-reduce.6
  395.7 39.1 all-reduce.8
  470.8 37.3 all-reduce.10
where the time goes:
time: 794 us; the launch traced here: 786 us
  waiting for transfers between devices  427 us (54%)
  matrix products  225 us (28%)
  other arithmetic  48.4 us (6%)
  local copies, waits for them, and re-layouts  40 us (5%)
  starting transfers between devices  20.4 us (3%)
  between operations  15.6 us (2%)
  loops' own time  10.5 us (1%)
    all_gather x1, waiting for transfers between devices, on_device(): lax.all_gather(w_up[0], 'dp', axis=0, tiled=True)  109 us
    all_gather x1, waiting for transfers between devices, on_device(): lax.all_gather(w_down[0], 'dp', axis=0, tiled=True)  98.5 us
    psum x2, waiting for transfers between devices, forward_layer(): lax.psum(partial_value.astype(jnp.bfloat16), 'mp').astype(jnp.float32)  75.3 us
    psum x2, waiting for transfers between devices, backward_layer(): lax.psum(partial_value.astype(jnp.bfloat16), 'mp').astype(jnp.float32)  60.1 us
    all_to_all x1, waiting for transfers between devices, on_device(): lax.all_to_all(grad_slots, 'dp', split_axis=1, concat_axis=0, tiled=True)  41.7 us
    ppermute x4, waiting for transfers between devices, passed_along(): return lax.ppermute(block, axis, route)  40.3 us
    dot_general x2, matrix products, backward_layer(): lax.dot_general(grad_pre, up_rows, (((1,), (1,)), ((), ())), preferred_el...  31.5 us
    dot_general x12, matrix products, inverse_root(): iterate = jnp.dot(iterate, step_mat, precision=highest)  29.8 us
  transfers between devices with their start and end apart: 12, of which 11 were waited for; matrix products, arithmetic and copies ran while one was open for 6% of the time, Pallas kernels for 0%

commit v1 on v0

--- a/solution.py
+++ b/solution.py
@@ -10,6 +10,29 @@
 decay_rate = 0.9
 ridge_shift = 0.001
 highest = lax.Precision.HIGHEST
+
+
+def joined_along(parts, dim):
+    shape = list(parts.shape[1:])
+    shape[dim] *= parts.shape[0]
+    return jnp.moveaxis(parts, 0, dim).reshape(shape)
+
+
+def collected_by_bits(x, axis):
+    devices, index = (lax.axis_size(axis), lax.axis_index(axis))
+    pieces, bit = (x[None], 1)
+    while bit < devices:
+        received = lax.ppermute(pieces, axis, [(i, i ^ bit) for i in range(devices)])
+        low = index & bit == 0
+        pieces = jnp.concatenate(
+            [jnp.where(low, pieces, received), jnp.where(low, received, pieces)]
+        )
+        bit *= 2
+    return pieces
+
+
+def doubled_up(array, axis, dim):
+    return joined_along(collected_by_bits(array, axis), dim)
 
 
 def passed_along(block, axis, distance):
@@ -97,7 +120,7 @@
     micro_count, row_count, model_width = activations.shape
     gain_row = norm_gain[0]
     up_full, down_full = (
-        lax.all_gather(w_up[0], "dp", axis=0, tiled=True),
+        doubled_up(w_up[0], "dp", 0),
         lax.all_gather(w_down[0], "dp", axis=0, tiled=True),
     )
     shard_ff = up_full.shape[1]

time: 794 us -> 883 us (1.11)
  waiting for transfers between devices: 427 us -> 487 us
  other arithmetic: 48.4 us -> 71.7 us
    ppermute x0 -> x2, waiting for transfers between devices: none -> 269 us  [collected_by_bits(): lax.ppermute(pieces, axis, [(i, i ^ bit) for i in range(devices)])]
    all_gather x1 -> x0, waiting for transfers between devices: 109 us -> none  [on_device(): lax.all_gather(w_up[0], 'dp', axis=0, tiled=True)]
    all_gather x1, waiting for transfers between devices: 98.5 us -> 0.02 us  [on_device(): lax.all_gather(w_down[0], 'dp', axis=0, tiled=True)]
    select_n x0 -> x2, other arithmetic: none -> 12.6 us  [collected_by_bits(): jnp.where(low, pieces, received)]
    concatenate x0 -> x2, other arithmetic: none -> 10.7 us  [collected_by_bits(): jnp.concatenate([jnp.where(low, pieces, received), jnp.where(low, receive...]
  transfers between devices with their start and end apart: 12 -> 13, of which waited for: 11 -> 11; matrix products, arithmetic and copies ran while one was open for 6% -> 8% of each run, Pallas kernels for 0% -> 0%
where the time goes in v1:
time: 883 us; the launch traced here: 874 us
  waiting for transfers between devices  487 us (55%)
  matrix products  220 us (25%)
  other arithmetic  71.7 us (8%)
  local copies, waits for them, and re-layouts  45.7 us (5%)
  starting transfers between devices  24 us (3%)
  between operations  15.3 us (2%)
  loops' own time  10.4 us (1%)
    ppermute x2, waiting for transfers between devices, collected_by_bits(): lax.ppermute(pieces, axis, [(i, i ^ bit) for i in range(devices)])  269 us
    psum x2, waiting for transfers between devices, forward_layer(): lax.psum(partial_value.astype(jnp.bfloat16), 'mp').astype(jnp.float32)  75.3 us
    psum x2, waiting for transfers between devices, backward_layer(): lax.psum(partial_value.astype(jnp.bfloat16), 'mp').astype(jnp.float32)  60.2 us
    all_to_all x1, waiting for transfers between devices, on_device(): lax.all_to_all(grad_slots, 'dp', split_axis=1, concat_axis=0, tiled=True)  41.7 us
    ppermute x4, waiting for transfers between devices, passed_along(): return lax.ppermute(block, axis, route)  40.3 us
    dot_general x2, matrix products, backward_layer(): lax.dot_general(grad_pre, up_rows, (((1,), (1,)), ((), ())), preferred_el...  31.5 us
    dot_general x12, matrix products, inverse_root(): iterate = jnp.dot(iterate, step_mat, precision=highest)  29.8 us
    dot_general x2, matrix products, forward_layer(): lax.dot_general(hidden, down_rows, (((1,), (1,)), ((), ())), preferred_el...  24.1 us
  transfers between devices with their start and end apart: 13, of which 11 were waited for; matrix products, arithmetic and copies ran while one was open for 8% of the time, Pallas kernels for 0%

profile of v1, /device:TPU:0, one launch (start us, length us, event | category | flops | bytes accessed | tf_op | source)
XLA Modules:
  0.0 874.4 jit_solution(6871640006053946199)
XLA Ops:
  8.5 7.1 collective-permute-done
  15.6 6.2 broadcast_select_fusion.3
  21.9 9.1 %pad_maximum_fusion.1 = bf16[2,1024,2048]{2,1,0:T(8,128)(2,1)} fusion(bf16[1,1024,2048]{2,1,0:T(8,128)(2,1)} %get-tuple-element.160, bf16[1,1024,2048]{2,1,0:T(8,128)(2,1)S(1)} %get-tuple-element.159), kind=kLoop, calls=%fused_computation.112 | loop fusion | flops 4194304 | bytes 16777216 | tf_op jit(solution)/shard_map/concatenate | solution.py:27
  34.3 261.6 %collective-permute-done.1 = bf16[2,1024,2048]{2,1,0:T(8,128)(2,1)} collective-permute-done((bf16[2,1024,2048]{2,1,0:T(8,128)(2,1)}, bf16[2,1024,2048]{2,1,0:T(8,128)(2,1)}, u32[]{:S(2)}, u32[]{:S(2)}) %collective-permute-start.1) | collective-permute-done | bytes 8388640 | tf_op jit(solution)/shard_map/ppermute | solution.py:25
  295.9 6.3 broadcast_select_fusion.1
  303.9 5.7 copy-done
  309.6 4.3 bitcast_dynamic-update-slice_fusion.1
  313.9 11.9 %fusion.92 = bf16[64,4096]{1,0:T(8,128)(2,1)} fusion(bf16[1,4096,2048]{2,1,0:T(8,128)(2,1)} %all-gather.3.cloned.1.call-done, f32[64,2048]{1,0:T(8,128)S(1)} %get-tuple-element.169), kind=kOutput, calls=%fused_computation.124 | convolution fusion | flops 1074659328 | bytes 17825792 | tf_op jit(solution)/shard_map/dot_general | solution.py:75
  325.9 38.7 %all-reduce.5.cloned.1.call-done = bf16[64,4096]{1,0:T(8,128)(2,1)} async-done(((bf16[64,4096]{1,0:T(8,128)(2,1)}), bf16[64,4096]{1,0:T(8,128)(2,1)}) %all-reduce.5.cloned.1.call-update) | async-done | bytes 524304 | tf_op jit(solution)/shard_map/psum | solution.py:78
  365.8 3.6 collective-permute-start.2
  369.7 9.8 %collective-permute-done.2 = bf16[64,4096]{1,0:T(8,128)(2,1)S(1)} collective-permute-done((bf16[64,4096]{1,0:T(8,128)(2,1)S(1)}, bf16[64,4096]{1,0:T(8,128)(2,1)S(1)}, u32[]{:S(2)}, u32[]{:S(2)}) %collective-permute-start.2) | collective-permute-done | bytes 524320 | tf_op jit(solution)/shard_map/ppermute | solution.py:41
  379.9 9.7 %fusion.187 = (bf16[2,64,2048]{2,1,0:T(8,128)(2,1)S(1)}, f32[64,2048]{1,0:T(8,128)}) fusion(bf16[2,64,2048]{2,1,0:T(8,128)(2,1)S(1)} %get-tuple-element.168, s32[]{:T(128)S(6)} %min.20, pred[]{:T(512)S(6)} %and.72, bf16[4096,2048]{1,0:T(8,128)(2,1)} %bitcast.225, bf16[64,4096]{1,0:T(8,128)(2,1)S(1)} %get-tuple-element.148, f32[4096]{0:T(1024)S(1)} %bitcast.234, ...), kind=kOutput, calls=%fused_computation.235 | convolution fusion | flops 1075576832 | bytes 18366980 | tf_op jit(solution)/shard_map/dot_general | solution.py:73
  389.6 12.1 %fusion.95 = bf16[64,4096]{1,0:T(8,128)(2,1)} fusion(bf16[1,4096,2048]{2,1,0:T(8,128)(2,1)} %all-gather.3.cloned.1.call-done, f32[64,2048]{1,0:T(8,128)} %get-tuple-element.171), kind=kOutput, calls=%fused_computation.125 | convolution fusion | flops 1074659328 | bytes 17825792 | tf_op jit(solution)/shard_map/dot_general | solution.py:75
  404.6 36.6 %all-reduce.7.cloned.1.call-done = bf16[64,4096]{1,0:T(8,128)(2,1)} async-done(((bf16[64,4096]{1,0:T(8,128)(2,1)}), bf16[64,4096]{1,0:T(8,128)(2,1)}) %all-reduce.7.cloned.1.call-update) | async-done | bytes 524304 | tf_op jit(solution)/shard_map/psum | solution.py:78
  442.4 3.7 collective-permute-start.3
  451.0 5.0 collective-permute-done.3
  456.5 9.0 %fusion.186 = (bf16[2,64,2048]{2,1,0:T(8,128)(2,1)S(1)}, f32[64,2048]{1,0:T(8,128)S(1)}) fusion(bf16[2,64,2048]{2,1,0:T(8,128)(2,1)S(1)} %copy-done.7, s32[]{:T(128)S(6)} %min.21, pred[]{:T(512)S(6)} %and.73, bf16[4096,2048]{1,0:T(8,128)(2,1)} %bitcast.226, bf16[64,4096]{1,0:T(8,128)(2,1)S(1)} %get-tuple-element.146, f32[64]{0:T(128)S(1)} %add_rsqrt_fusion, ...), kind=kOutput, calls=%fused_computation.233 | convolution fusion | flops 1075576832 | bytes 18366980 | tf_op jit(solution)/shard_map/dot_general | solution.py:73
  468.2 15.7 %convolution_convert_fusion.4 = bf16[64,4096]{1,0:T(8,128)(2,1)} fusion(bf16[4096,2048]{1,0:T(8,128)(2,1)} %bitcast.227, bf16[1,4096,2048]{2,1,0:T(8,128)(2,1)} %all-gather.3.cloned.1.call-done, f32[2,64,2048]{2,1,0:T(8,128)} %fusion.170, s32[]{:T(128)S(6)} %min.22, bf16[2,64,4096]{2,1,0:T(8,128)(2,1)S(1)} %copy-done.5, pred[]{:T(512)S(6)} %eq.68), kind=kOutput, calls=%fused_computation.123 | convolution fusion | flops 2149187584 | bytes 35127300 | tf_op jit(solution)/shard_map/dot_general | solution.py:86
  486.0 37.3 %all-reduce.9.cloned.1.call-done = bf16[64,4096]{1,0:T(8,128)(2,1)} async-done(((bf16[64,4096]{1,0:T(8,128)(2,1)}), bf16[64,4096]{1,0:T(8,128)(2,1)}) %all-reduce.9.cloned.1.call-update) | async-done | bytes 524304 | tf_op jit(solution)/shard_map/psum | solution.py:89
  528.8 12.2 %collective-permute-done.4 = bf16[64,4096]{1,0:T(8,128)(2,1)} collective-permute-done((bf16[64,4096]{1,0:T(8,128)(2,1)S(1)}, bf16[64,4096]{1,0:T(8,128)(2,1)}, u32[]{:S(2)}, u32[]{:S(2)}) %collective-permute-start.4) | collective-permute-done | bytes 524320 | tf_op jit(solution)/shard_map/ppermute | solution.py:41
  543.3 15.8 %convolution_convert_fusion.3 = bf16[64,4096]{1,0:T(8,128)(2,1)} fusion(bf16[4096,2048]{1,0:T(8,128)(2,1)} %bitcast.228, bf16[64,4096]{1,0:T(8,128)(2,1)S(1)} %get-tuple-element.144, bf16[1,4096,2048]{2,1,0:T(8,128)(2,1)} %all-gather.3.cloned.1.call-done, f32[2,64,2048]{2,1,0:T(8,128)} %fusion.170, s32[]{:T(128)S(6)} %min.23), kind=kOutput, calls=%fused_computation.122 | convolution fusion | flops 2148925440 | bytes 35127300 | tf_op jit(solution)/shard_map/dot_general | solution.py:86
  564.2 4.7 select_bitcast_fusion.1
  568.9 4.8 all-to-all-start
  573.7 22.9 %all-reduce.11.cloned.1.call-done = bf16[64,4096]{1,0:T(8,128)(2,1)} async-done(((bf16[64,4096]{1,0:T(8,128)(2,1)}), bf16[64,4096]{1,0:T(8,128)(2,1)}) %all-reduce.11.cloned.1.call-update) | async-done | bytes 524304 | tf_op jit(solution)/shard_map/psum | solution.py:89
  600.7 13.3 %collective-permute-done.5 = bf16[64,4096]{1,0:T(8,128)(2,1)S(1)} collective-permute-done((bf16[64,4096]{1,0:T(8,128)(2,1)S(1)}, bf16[64,4096]{1,0:T(8,128)(2,1)S(1)}, u32[]{:S(2)}, u32[]{:S(2)}) %collective-permute-start.5) | collective-permute-done | bytes 524320 | tf_op jit(solution)/shard_map/ppermute | solution.py:41
  620.8 4.7 select_bitcast_fusion
  625.5 5.0 all-to-all-start.1
  630.6 6.4 copy.34
  637.0 41.7 %all-to-all-done.1 = bf16[128,32,512]{2,0,1:T(8,128)(2,1)} async-done(((bf16[128,32,512]{2,0,1:T(8,128)(2,1)}), bf16[128,32,512]{2,0,1:T(8,128)(2,1)}, u32[]{:S(2)}, u32[]{:S(2)}) %all-to-all-start.1) | async-done | bytes 4194336 | tf_op jit(solution)/shard_map/all_to_all | solution.py:177
  678.7 10.9 %convolution_convert_fusion.2 = bf16[4,8,512,512]{3,2,1,0:T(8,128)(2,1)} fusion(bf16[4,128,8,512]{1,3,2,0:T(8,128)(2,1)} %bitcast.231, bf16[4,128,8,512]{3,1,2,0:T(8,128)(2,1)} %bitcast.37), kind=kOutput, calls=%fused_computation.111 | convolution fusion | flops 2155872256 | bytes 25165824 | tf_op jit(solution)/shard_map/snbk,snbl->sbkl/dot_general | solution.py:181
  689.6 9.6 %convert_reduce_fusion = f32[8,512,512]{2,1,0:T(8,128)S(1)} fusion(bf16[4,8,512,512]{3,2,1,0:T(8,128)(2,1)} %convolution_convert_fusion.2), kind=kLoop, calls=%fused_computation.101 | loop fusion | flops 14680064 | bytes 25165824 | tf_op jit(solution)/shard_map/reduce_sum | solution.py:183
  699.2 19.7 %bitcast_add_fusion = f32[8,512,512]{2,1,0:T(8,128)} fusion(f32[1,8,512,512]{3,2,1,0:T(8,128)} %param.22, f32[8,512,512]{2,1,0:T(8,128)S(1)} %convert_reduce_fusion), kind=kOutput, calls=%fused_computation.113 | convolution fusion | flops 12893290496 | bytes 25165824 | tf_op jit(solution)/shard_map/sji,sjk->sik/dot_general | solution.py:191
  718.9 17.6 %bitcast_add_fusion.1 = f32[8,512,512]{2,1,0:T(8,128)} fusion(f32[1,8,512,512]{3,2,1,0:T(8,128)} %param.21, f32[8,512,512]{2,1,0:T(8,128)S(1)} %convert_reduce_fusion), kind=kOutput, calls=%fused_computation.114 | convolution fusion | flops 12893290496 | bytes 25165824 | tf_op jit(solution)/shard_map/sij,skj->sik/dot_general | solution.py:187
  736.5 118.7 %while.12 = (s32[]{:T(128)}, bf16[8,512,512]{2,1,0:T(8,128)(2,1)}, bf16[8,512,512]{2,1,0:T(8,128)(2,1)}, pred[8]{0:T(512)(128)(4,1)S(1)}, bf16[8,512,512]{2,1,0:...) while((s32[]{:T(128)}, bf16[8,512,512]{2,1,0:T(8,128)(2,1)}, ...), condition=%wide.region_18.19_spmd, body=%wide.region_13.18_spmd.sunk | while | flops 16121331712 | bytes 28315412 | solution.py:212
  748.7 31.2 %conditional.2 = (bf16[1,512,512]{2,1,0:T(8,128)(2,1)S(1)}, bf16[1,512,512]{2,1,0:T(8,128)(2,1)S(1)}) conditional(s32[]{:T(128)} %bitcast.220, (bf16[8,512,512]{2,1,0:T(8,128)(2,1)}, s32[]{:T(128)}, bf16[8,512,512]{2,1,0:T(8,128)(2,1)}) %tuple.67, (f32[8,512,512]{2,1,0:T(8,128)}, s32[]{:T(128)}, f32[8,512,512]{2,1,0:T(8,128)}) %tuple.68), branch_computations={%region_14.14_spmd, %region_15.17_spmd} | conditional | flops 16121331712 | bytes 26217596 | solution.py:202
  751.9 3.6 fusion.6
  760.5 3.1 fusion.15
  766.2 3.7 fusion.3
  771.7 3.1 select_subtract_fusion.2
  782.2 31.1 %conditional.2 = (bf16[1,512,512]{2,1,0:T(8,128)(2,1)S(1)}, bf16[1,512,512]{2,1,0:T(8,128)(2,1)S(1)}) conditional(s32[]{:T(128)} %bitcast.220, (bf16[8,512,512]{2,1,0:T(8,128)(2,1)}, s32[]{:T(128)}, bf16[8,512,512]{2,1,0:T(8,128)(2,1)}) %tuple.67, (f32[8,512,512]{2,1,0:T(8,128)}, s32[]{:T(128)}, f32[8,512,512]{2,1,0:T(8,128)}) %tuple.68), branch_computations={%region_14.14_spmd, %region_15.17_spmd} | conditional | flops 16121331712 | bytes 26217596 | solution.py:202
  785.4 3.6 fusion.6
  790.9 3.1 select_subtract_fusion
  799.7 3.6 fusion.3
  815.6 31.1 %conditional.2 = (bf16[1,512,512]{2,1,0:T(8,128)(2,1)S(1)}, bf16[1,512,512]{2,1,0:T(8,128)(2,1)S(1)}) conditional(s32[]{:T(128)} %bitcast.220, (bf16[8,512,512]{2,1,0:T(8,128)(2,1)}, s32[]{:T(128)}, bf16[8,512,512]{2,1,0:T(8,128)(2,1)}) %tuple.67, (f32[8,512,512]{2,1,0:T(8,128)}, s32[]{:T(128)}, f32[8,512,512]{2,1,0:T(8,128)}) %tuple.68), branch_computations={%region_14.14_spmd, %region_15.17_spmd} | conditional | flops 16121331712 | bytes 26217596 | solution.py:202
  818.8 3.6 fusion.6
  833.1 3.6 fusion.3
  841.7 3.1 fusion.14
  855.2 12.3 %convert_bitcast_fusion = bf16[1,8,512,512]{3,2,1,0:T(8,128)(2,1)} fusion(bf16[8,512,512]{2,1,0:T(8,128)(2,1)} %get-tuple-element.120, bf16[8,512,512]{2,1,0:T(8,128)(2,1)} %get-tuple-element.121, f32[8,512,512]{2,1,0:T(8,128)} %copy-done.1), kind=kOutput, calls=%fused_computation.129 | convolution fusion | flops 4303355904 | bytes 20971520 | tf_op jit(solution)/shard_map/sij,sjk->sik/dot_general | solution.py:219
  (143 shorter events, 125.9 us)
Async XLA Ops:
  7.2 306.7 %all-gather.3.cloned.1.call-start = ((), (), s32[]{:S(2)}) async-start(), calls=%async_computation.6 | async-start | bytes 20971520 | tf_op jit(solution)/shard_map/all_gather | solution.py:124
  7.9 356.7 %all-reduce.5.cloned.1.call-start = ((), (), s32[]{:S(2)}) async-start(), calls=%async_computation.2 | async-start | bytes 1048576 | tf_op jit(solution)/shard_map/psum | solution.py:78
  7.9 7.7 collective-permute-start
  21.9 9.1 %copy-start.2 = (bf16[1,1024,2048]{2,1,0:T(8,128)(2,1)}, bf16[1,1024,2048]{2,1,0:T(8,128)(2,1)S(1)}, u32[]{:S(2)}) copy-start(bf16[1,1024,2048]{2,1,0:T(8,128)(2,1)S(1)} %get-tuple-element.159) | copy-start | bytes 12582916
  21.9 12.2 %copy-start.3 = (bf16[2,64,4096]{2,1,0:T(8,128)(2,1)S(1)}, bf16[2,64,4096]{2,1,0:T(8,128)(2,1)}, u32[]{:S(2)}) copy-start(bf16[2,64,4096]{2,1,0:T(8,128)(2,1)} %param.16) | copy-start | bytes 3145732
  31.0 264.9 %collective-permute-start.1 = (bf16[2,1024,2048]{2,1,0:T(8,128)(2,1)}, bf16[2,1024,2048]{2,1,0:T(8,128)(2,1)}, u32[]{:S(2)}, u32[]{:S(2)}) collective-permute-start(bf16[2,1024,2048]{2,1,0:T(8,128)(2,1)} %pad_maximum_fusion.1), channel_id=1, source_target_pairs={{0,8},{4,12},{8,0},{12,4},{1,9},{5,13},{9,1},{13,5},{2,10},{6,14},... | collective-permute-start | bytes 25165832 | tf_op jit(solution)/shard_map/ppermute | solution.py:25
  302.2 7.3 copy-start.11
  303.8 5.7 copy-start
  313.8 12.0 %copy-start.10 = (f32[64,2048]{1,0:T(8,128)}, f32[64,2048]{1,0:T(8,128)S(1)}, u32[]{:S(2)}) copy-start(f32[64,2048]{1,0:T(8,128)S(1)} %get-tuple-element.169) | copy-start | bytes 1572868
  313.9 50.8 %copy-start.4 = (bf16[2,64,4096]{2,1,0:T(8,128)(2,1)S(1)}, bf16[2,64,4096]{2,1,0:T(8,128)(2,1)}, u32[]{:S(2)}) copy-start(bf16[2,64,4096]{2,1,0:T(8,128)(2,1)} %param.16) | copy-start | bytes 3145732
  325.8 115.3 %all-reduce.7.cloned.1.call-start = ((), (), s32[]{:S(2)}) async-start(), calls=%async_computation.3 | async-start | bytes 1048576 | tf_op jit(solution)/shard_map/psum | solution.py:78
  365.8 13.6 %collective-permute-start.2 = (bf16[64,4096]{1,0:T(8,128)(2,1)S(1)}, bf16[64,4096]{1,0:T(8,128)(2,1)S(1)}, u32[]{:S(2)}, u32[]{:S(2)}) collective-permute-start(bf16[64,4096]{1,0:T(8,128)(2,1)S(1)} %fusion.129), channel_id=1, source_target_pairs={{0,16},{1,17},{2,18},{3,19},{4,20},{5,21},{6,22},{7,23},{8,24},{9,... | collective-permute-start | bytes 1572872 | tf_op jit(solution)/shard_map/ppermute | solution.py:41
  389.6 13.2 %copy-start.6 = (bf16[2,64,2048]{2,1,0:T(8,128)(2,1)}, bf16[2,64,2048]{2,1,0:T(8,128)(2,1)S(1)}, u32[]{:S(2)}) copy-start(bf16[2,64,2048]{2,1,0:T(8,128)(2,1)S(1)} %get-tuple-element.170) | copy-start | bytes 1572868
  389.6 12.9 %copy-start.12 = (s32[2,16,8]{1,2,0:T(8,128)S(1)}, s32[2,16,8]{1,2,0:T(8,128)}, u32[]{:S(2)}) copy-start(s32[2,16,8]{1,2,0:T(8,128)} %param.26) | copy-start | bytes 3076
  389.6 12.9 %copy-start.13 = (s32[2,16,8]{1,2,0:T(8,128)S(1)}, s32[2,16,8]{1,2,0:T(8,128)}, u32[]{:S(2)}) copy-start(s32[2,16,8]{1,2,0:T(8,128)} %param.25) | copy-start | bytes 3076
  401.8 121.5 %all-reduce.9.cloned.1.call-start = ((), (), s32[]{:S(2)}) async-start(), calls=%async_computation.4 | async-start | bytes 1048576 | tf_op jit(solution)/shard_map/psum | solution.py:89
  441.1 15.3 %copy-start.7 = (bf16[2,64,2048]{2,1,0:T(8,128)(2,1)S(1)}, bf16[2,64,2048]{2,1,0:T(8,128)(2,1)}, u32[]{:S(2)}) copy-start(bf16[2,64,2048]{2,1,0:T(8,128)(2,1)} %copy-done.6) | copy-start | bytes 1572868
  442.4 13.6 %collective-permute-start.3 = (bf16[64,4096]{1,0:T(8,128)(2,1)S(1)}, bf16[64,4096]{1,0:T(8,128)(2,1)S(1)}, u32[]{:S(2)}, u32[]{:S(2)}) collective-permute-start(bf16[64,4096]{1,0:T(8,128)(2,1)S(1)} %fusion.138), channel_id=1, source_target_pairs={{0,16},{1,17},{2,18},{3,19},{4,20},{5,21},{6,22},{7,23},{8,24},{9,... | collective-permute-start | bytes 1572872 | tf_op jit(solution)/shard_map/ppermute | solution.py:41
  456.5 11.8 %copy-start.5 = (bf16[2,64,4096]{2,1,0:T(8,128)(2,1)S(1)}, bf16[2,64,4096]{2,1,0:T(8,128)(2,1)}, u32[]{:S(2)}) copy-start(bf16[2,64,4096]{2,1,0:T(8,128)(2,1)} %param.17) | copy-start | bytes 3145732
  465.5 0.8 copy-start.8
  484.0 112.7 %all-reduce.11.cloned.1.call-start = ((), (), s32[]{:S(2)}) async-start(), calls=%async_computation.5 | async-start | bytes 1048576 | tf_op jit(solution)/shard_map/psum | solution.py:89
  526.3 14.7 %collective-permute-start.4 = (bf16[64,4096]{1,0:T(8,128)(2,1)S(1)}, bf16[64,4096]{1,0:T(8,128)(2,1)}, u32[]{:S(2)}, u32[]{:S(2)}) collective-permute-start(bf16[64,4096]{1,0:T(8,128)(2,1)S(1)} %fusion.140), channel_id=1, source_target_pairs={{16,0},{17,1},{18,2},{19,3},{20,4},{21,5},{22,6},{23,7},{24,8},{25... | collective-permute-start | bytes 1572872 | tf_op jit(solution)/shard_map/ppermute | solution.py:41
  543.3 15.8 %copy-start.9 = (bf16[2,64,2048]{2,1,0:T(8,128)(2,1)S(1)}, bf16[2,64,2048]{2,1,0:T(8,128)(2,1)}, u32[]{:S(2)}) copy-start(bf16[2,64,2048]{2,1,0:T(8,128)(2,1)} %copy-done.8) | copy-start | bytes 1572868
  568.9 56.6 %all-to-all-start = ((bf16[128,32,512]{2,0,1:T(8,128)(2,1)}), bf16[128,32,512]{2,0,1:T(8,128)(2,1)}, u32[]{:S(2)}, u32[]{:S(2)}) async-start(bf16[128,32,512]{2,0,1:T(8,128)(2,1)} %select_bitcast_fusion.1), calls=%async_computation | async-start | bytes 8388608 | tf_op jit(solution)/shard_map/all_to_all | solution.py:176
  599.4 14.6 %collective-permute-start.5 = (bf16[64,4096]{1,0:T(8,128)(2,1)S(1)}, bf16[64,4096]{1,0:T(8,128)(2,1)S(1)}, u32[]{:S(2)}, u32[]{:S(2)}) collective-permute-start(bf16[64,4096]{1,0:T(8,128)(2,1)S(1)} %fusion.142), channel_id=1, source_target_pairs={{16,0},{17,1},{18,2},{19,3},{20,4},{21,5},{22,6},{23,7},{24,8},{25... | collective-permute-start | bytes 1572872 | tf_op jit(solution)/shard_map/ppermute | solution.py:41
  625.5 53.2 %all-to-all-start.1 = ((bf16[128,32,512]{2,0,1:T(8,128)(2,1)}), bf16[128,32,512]{2,0,1:T(8,128)(2,1)}, u32[]{:S(2)}, u32[]{:S(2)}) async-start(bf16[128,32,512]{2,0,1:T(8,128)(2,1)} %select_bitcast_fusion), calls=%async_computation.1 | async-start | bytes 8388608 | tf_op jit(solution)/shard_map/all_to_all | solution.py:177
  699.2 19.7 %copy-start.1 = (f32[8,512,512]{2,1,0:T(8,128)}, f32[8,512,512]{2,1,0:T(8,128)S(1)}, u32[]{:S(2)}) copy-start(f32[8,512,512]{2,1,0:T(8,128)S(1)} %convert_reduce_fusion) | copy-start | bytes 25165828
Sparse Core Ops, SparseCore 0:
  9.5 189.4 all-gather.2
  326.0 38.6 all-reduce.4
  401.9 39.1 all-reduce.6
  484.1 39.1 all-reduce.8
  559.2 37.4 all-reduce.10
